TPU v7x, 32 devices: a whole 2x2x4 slice. The times are simulated.
32 devices in a mesh: tm: 8 (over z, x), lat: 4 (over y, core).
Axes of the slice: x: 2, y: 2, z: 4, core: 2. Of those that a mesh axis runs over, the one named last changes fastest.
Arguments:
- states: float32 [8, 3, 32, 2048], P('tm', None, 'lat'), may hold values from -1.5 to 1.5
- background: float32 [3, 32, 2048], P(None, 'lat'), may hold values from -1.5 to 1.5
- error_std: float32 [3, 32, 2048], P(None, 'lat'), may hold values from 0.5 to 2
- land_mask: int32 [8, 128], P('lat'), may hold values 0 or 1
- obs_cells: int32 [8, 512], P('tm', 'lat'), may hold values from 0 to 16383
- measurement_moments: int32 [8, 512], P('tm', 'lat'), may hold values from 0 to 3
- obs_values: float32 [8, 512], P('tm', 'lat'), may hold values from -2.4 to 2.4
- obs_error: float32 [8, 512], P('tm', 'lat'), may hold values from 0.3 to 1
Outputs:
- estimated_openings: float32 [8, 3, 32, 2048], P('tm', None, 'lat')
- slid: float32 [8, 3, 32, 2048], P('tm', None, 'lat')
- costs: float32 [2], replicated
Inputs may be any that keep to these rules, and one draw needn't show every extreme that they name: `obs_cells`: cell index within the band: row within the band times 2048 plus column. `land_mask`: each entry covers 4 x 16 cells.
All inputs are finite; a program needn't handle non-finite values. No bound on the sum of `land_mask` on one device may be relied on, other than what follows from the above.
Results may differ from a plain program's by a relative error of at most 0.0003.
Values sent between devices are 32-bit elements; how exact they have to be, the bound alone decides.
A program may use at most 64 MiB of HBM per device.

v0:
```python
import jax
import jax.numpy as jnp
from jax import lax
from jax.sharding import PartitionSpec as P

STEPS = 4
ITERS = 2
TILE_LAT = 4
TILE_LON = 16


TIME_STEP = 0.25
MEAN_DEPTH = 1.0
GRAVITY = 1.0
DRAG_RATE = 0.02
STEP_LENGTH = 0.3
CORIOLIS_MEAN = 0.3
CORIOLIS_SLOPE = 0.2
EPSILON = 1e-06


def extended_2(cells, sides, width):
    for axis, dim in sides:
        count = lax.axis_size(axis)
        ends = count - 1
        head = lax.slice_in_dim(cells, 0, width, axis=dim)
        tail = lax.slice_in_dim(cells, cells.shape[dim] - width, cells.shape[dim], axis=dim)
        cells = jnp.concatenate(
            [
                lax.ppermute(tail, axis, [(i, (i + 1) % count) for i in range(ends)]),
                cells,
                lax.ppermute(head, axis, [((i + 1) % count, i) for i in range(ends)]),
            ],
            axis=dim,
        )
    return cells


def passed_along(x, axis, by):
    devices = lax.axis_size(axis)
    pairs = [(i, i + by) for i in range(devices) if 0 <= i + by < devices]
    return lax.ppermute(x, axis, pairs)


def expand_mask(land_mask):
    tiles_lat, tiles_lon = land_mask.shape
    grown = jnp.broadcast_to(
        land_mask[:, None, :, None], (tiles_lat, TILE_LAT, tiles_lon, TILE_LON)
    )
    return grown.reshape(tiles_lat * TILE_LAT, tiles_lon * TILE_LON).astype(jnp.float32)


def zonal_diff(field):
    return 0.5 * (jnp.roll(field, -1, axis=1) - jnp.roll(field, 1, axis=1))


def merid_diff(field):
    return 0.5 * (field[2:] - field[:-2])


def model_step(padded, coriolis, ocean_mask):
    interior = padded[:, 1:-1]
    height, eastward, northward = (interior[0], interior[1], interior[2])
    height_pad, east_pad, north_pad = (padded[0], padded[1], padded[2])
    d_height = -(
        zonal_diff((MEAN_DEPTH + height) * eastward)
        + merid_diff((MEAN_DEPTH + height_pad) * north_pad)
    )
    d_east = (
        coriolis * northward
        - GRAVITY * zonal_diff(height)
        - eastward * zonal_diff(eastward)
        - northward * merid_diff(east_pad)
        - DRAG_RATE * eastward
    )
    d_north = (
        -coriolis * eastward
        - GRAVITY * merid_diff(height_pad)
        - eastward * zonal_diff(northward)
        - northward * merid_diff(north_pad)
        - DRAG_RATE * northward
    )
    return interior + TIME_STEP * ocean_mask * jnp.stack([d_height, d_east, d_north])


def shards(
    states, background, error_std, land_mask, obs_cells, measurement_moments, obs_values, obs_error
):
    band_rows = background.shape[1]
    lon_cells = background.shape[2]
    total_rows = band_rows * lax.axis_size("lat")
    first_row = lax.axis_index("lat") * band_rows
    ocean_mask = expand_mask(land_mask)
    variance = error_std * error_std
    cell_ids = obs_cells[0]
    obs_times = measurement_moments[0]
    targets = obs_values[0]
    precision = 1.0 / (obs_error[0] * obs_error[0])
    cell_count = 3 * total_rows * lon_cells
    window_count = lax.axis_size("tm")
    sub_index = lax.axis_index("tm")
    is_first = sub_index == 0
    is_last = sub_index == window_count - 1
    wide_rows = first_row - STEPS + jnp.arange(band_rows + 2 * STEPS, dtype=jnp.int32)
    wide_lat = wide_rows.astype(jnp.float32)[:, None]
    wide_coriolis = CORIOLIS_MEAN + CORIOLIS_SLOPE * (wide_lat / total_rows - 0.5)
    inside = ((wide_rows >= 0) & (wide_rows < total_rows)).astype(jnp.float32)[:, None]
    wide_ocean = extended_2(ocean_mask[None], (("lat", 1),), STEPS)[0]

    def deep_run(extended):
        current = extended
        measured_quantities = jnp.zeros(cell_ids.shape, jnp.float32)
        for substep in range(STEPS):
            reach = STEPS - substep
            inner = current[:, reach : reach + band_rows]
            values = jnp.take(inner[0].reshape(-1), cell_ids)
            measured_quantities = measured_quantities + jnp.where(obs_times == substep, values, 0.0)
            rows_now = current.shape[1]
            low = substep + 1
            high = substep + rows_now - 1
            stepped = model_step(current, wide_coriolis[low:high], wide_ocean[low:high])
            current = stepped * inside[low:high]
        return (current, measured_quantities)

    def onward_integration(current):
        extended = extended_2(current, (("lat", 1),), STEPS)
        (final, measured_quantities), kept_trajectory_points = jax.vjp(deep_run, extended)
        return (final, measured_quantities, kept_trajectory_points)

    estimated_openings = states[0]
    costs = []
    for iteration in range(ITERS):
        predicted_closing_condition, measured_quantities, kept_trajectory_points = (
            onward_integration(estimated_openings)
        )
        misfit = measured_quantities - targets
        weighted = misfit * precision
        prior_gap = (estimated_openings - background) / variance
        reached_condition = passed_along(predicted_closing_condition, "tm", 1)
        own_term = jnp.where(
            is_first, prior_gap, (estimated_openings - reached_condition) / variance
        )
        returned = passed_along(own_term, "tm", -1)
        penalty = jnp.sum(own_term * own_term * variance)
        local_cost = 0.5 * (jnp.sum(misfit * weighted) + penalty)
        total_cost = lax.psum(local_cost, ("tm", "lat"))
        spread = kept_trajectory_points((-returned, weighted))[0]
        edges = extended_2(spread, (("lat", 1),), STEPS)
        adjoint = spread[:, STEPS : STEPS + band_rows]
        adjoint = adjoint.at[:, :STEPS].add(edges[:, :STEPS])
        adjoint = adjoint.at[:, band_rows - STEPS :].add(edges[:, edges.shape[1] - STEPS :])
        gradient = own_term + adjoint
        direction = variance * gradient
        local_steep = jnp.sum(gradient * direction)
        steepness = lax.psum(local_steep, ("tm", "lat"))
        step_scale = STEP_LENGTH / jnp.sqrt(steepness / (window_count * cell_count) + EPSILON)
        estimated_openings = estimated_openings - step_scale * direction
        costs.append(total_cost / cell_count)
    final_end, _, _ = onward_integration(estimated_openings)
    following = passed_along(estimated_openings, "tm", -1)
    slid = jnp.where(is_last, final_end, following)
    return (estimated_openings[None], slid[None], jnp.stack(costs))


def solution(mesh):
    placed = (
        P("tm", None, "lat", None),
        P(None, "lat", None),
        P(None, "lat", None),
        P("lat", None),
        P("tm", "lat"),
        P("tm", "lat"),
        P("tm", "lat"),
        P("tm", "lat"),
    )
    return jax.shard_map(
        shards,
        mesh=mesh,
        in_specs=placed,
        out_specs=(P("tm", None, "lat", None), P("tm", None, "lat", None), P()),
        check_vma=False,
    )
```

profile of v0, /device:TPU:9, one launch (start us, length us, event | category | flops | bytes accessed | tf_op | source)
XLA Modules:
  0.0 255.2 jit_solution(15714835527814559550)
XLA Ops:
  0.6 1.1 fusion.557
  1.7 3.7 %collective-permute-start = (f32[3,4,2048]{2,1,0:T(4,128)S(1)}, f32[3,4,2048]{2,1,0:T(4,128)S(1)}, u32[]{:S(2)}, u32[]{:S(2)}) collective-permute-start(f32[3,4,2048]{2,1,0:T(4,128)S(1)} %get-tuple-element.329), channel_id=1, source_target_pairs={{0,1},{1,2},{2,3},{4,5},{5,6},{6,7},{8,9},{9,10},{10,11},{12,13},{... | collective-permute-start | bytes 294920 | tf_op jit(solution)/shard_map/ppermute | solution.py:30
  5.4 1.9 collective-permute-start.1
  7.8 3.6 %collective-permute-start.2 = (f32[1,4,2048]{2,1,0:T(4,128)S(1)}, f32[1,4,2048]{2,1,0:T(4,128)S(1)}, u32[]{:S(2)}, u32[]{:S(2)}) collective-permute-start(f32[1,4,2048]{2,1,0:T(4,128)S(1)} %get-tuple-element.587), channel_id=1, source_target_pairs={{0,1},{1,2},{2,3},{4,5},{5,6},{6,7},{8,9},{9,10},{10,11},{12,13},{... | collective-permute-start | bytes 98312 | tf_op jit(solution)/shard_map/ppermute | solution.py:30
  11.4 1.9 collective-permute-start.3
  15.1 1.1 gather_fusion.1
  16.9 0.8 fusion.583
  20.4 0.8 fusion.587
  22.2 0.8 fusion.589
  26.1 0.8 fusion.593
  31.5 3.1 %collective-permute-start.4 = (f32[3,8,2048]{2,1,0:T(8,128)S(1)}, f32[3,8,2048]{2,1,0:T(8,128)S(1)}, u32[]{:S(2)}, u32[]{:S(2)}) collective-permute-start(f32[3,8,2048]{2,1,0:T(8,128)S(1)} %fusion.19), channel_id=1, source_target_pairs={{0,4},{4,8},{8,12},{12,16},{16,20},{20,24},{24,28},{1,5},{5,9},{9,... | collective-permute-start | bytes 589832 | tf_op jit(solution)/shard_map/ppermute | solution.py:42
  34.7 1.1 gather_fusion
  35.9 1.1 gather_fusion.3
  37.1 1.1 gather_fusion.2
  38.3 1.2 multiply_reduce_fusion.5
  39.6 3.1 %collective-permute-start.5 = (f32[3,8,2048]{2,1,0:T(8,128)S(1)}, f32[3,8,2048]{2,1,0:T(8,128)S(1)}, u32[]{:S(2)}, u32[]{:S(2)}) collective-permute-start(f32[3,8,2048]{2,1,0:T(8,128)S(1)} %divide_select_fusion.1), channel_id=1, source_target_pairs={{4,0},{8,4},{12,8},{16,12},{20,16},{24,20},{28,24},{5,1},{9,5},{13... | collective-permute-start | bytes 589832 | tf_op jit(solution)/shard_map/ppermute | solution.py:42
  42.6 1.3 scatter_custom_fusion
  43.9 1.3 scatter_custom_fusion.1
  45.3 1.3 scatter_custom_fusion.2
  46.6 1.5 scatter_custom_fusion.3
  64.0 3.8 %collective-permute-start.6 = (f32[3,4,2048]{2,1,0:T(4,128)S(1)}, f32[3,4,2048]{2,1,0:T(4,128)S(1)}, u32[]{:S(2)}, u32[]{:S(2)}) collective-permute-start(f32[3,4,2048]{2,1,0:T(4,128)S(1)} %get-tuple-element.279), channel_id=1, source_target_pairs={{0,1},{1,2},{2,3},{4,5},{5,6},{6,7},{8,9},{9,10},{10,11},{12,13},{... | collective-permute-start | bytes 294920 | tf_op jit(solution)/shard_map/ppermute | solution.py:30
  67.8 1.9 collective-permute-start.7
  69.8 3.9 %collective-permute-done.7 = f32[3,4,2048]{2,1,0:T(4,128)S(1)} collective-permute-done((f32[3,4,2048]{2,1,0:T(4,128)S(1)}, f32[3,4,2048]{2,1,0:T(4,128)S(1)}, u32[]{:S(2)}, u32[]{:S(2)}) %collective-permute-start.7) | collective-permute-done | bytes 98336 | tf_op jit(solution)/shard_map/ppermute | solution.py:32
  74.6 37.6 %psum.28 = f32[]{:T(128)} all-reduce(f32[]{:T(128)} %get-tuple-element.84), channel_id=1, replica_groups=mesh['tm'=8,'lat'=4] {'tm','lat'}, use_global_device_ids=true, to_apply=%region_5.7 | all-reduce | flops 1 | bytes 8 | tf_op jit(solution)/shard_map/psum | solution.py:155
  113.0 5.3 %collective-permute-start.8 = (f32[3,4,2048]{2,1,0:T(4,128)S(1)}, f32[3,4,2048]{2,1,0:T(4,128)S(1)}, u32[]{:S(2)}, u32[]{:S(2)}) collective-permute-start(f32[3,4,2048]{2,1,0:T(4,128)S(1)} %get-tuple-element.322), channel_id=1, source_target_pairs={{0,1},{1,2},{2,3},{4,5},{5,6},{6,7},{8,9},{9,10},{10,11},{12,13},{... | collective-permute-start | bytes 294920 | tf_op jit(solution)/shard_map/ppermute | solution.py:30
  118.3 1.9 collective-permute-start.9
  120.2 1.8 gather_fusion.5
  122.1 2.2 collective-permute-done.9
  127.8 0.8 fusion.569
  133.4 0.8 fusion.573
  145.0 2.8 %collective-permute-start.10 = (f32[3,8,2048]{2,1,0:T(8,128)}, f32[3,8,2048]{2,1,0:T(8,128)}, u32[]{:S(2)}, u32[]{:S(2)}) collective-permute-start(f32[3,8,2048]{2,1,0:T(8,128)} %fusion.18), channel_id=1, source_target_pairs={{0,4},{4,8},{8,12},{12,16},{16,20},{20,24},{24,28},{1,5},{5,9},{9,... | collective-permute-start | bytes 589832 | tf_op jit(solution)/shard_map/ppermute | solution.py:42
  147.9 1.3 gather_fusion.4
  149.2 1.3 gather_fusion.7
  150.5 1.3 gather_fusion.6
  153.1 1.0 divide_select_fusion
  154.1 3.3 %collective-permute-start.11 = (f32[3,8,2048]{2,1,0:T(8,128)S(1)}, f32[3,8,2048]{2,1,0:T(8,128)S(1)}, u32[]{:S(2)}, u32[]{:S(2)}) collective-permute-start(f32[3,8,2048]{2,1,0:T(8,128)S(1)} %divide_select_fusion), channel_id=1, source_target_pairs={{4,0},{8,4},{12,8},{16,12},{20,16},{24,20},{28,24},{5,1},{9,5},{13... | collective-permute-start | bytes 589832 | tf_op jit(solution)/shard_map/ppermute | solution.py:42
  157.5 1.4 scatter_custom_fusion.4
  158.9 1.6 scatter_custom_fusion.5
  160.6 1.4 scatter_custom_fusion.6
  162.0 1.4 scatter_custom_fusion.7
  179.9 2.4 collective-permute-start.12
  183.7 1.9 collective-permute-start.13
  185.7 3.9 %collective-permute-done.13 = f32[3,4,2048]{2,1,0:T(4,128)S(1)} collective-permute-done((f32[3,4,2048]{2,1,0:T(4,128)S(1)}, f32[3,4,2048]{2,1,0:T(4,128)S(1)}, u32[]{:S(2)}, u32[]{:S(2)}) %collective-permute-start.13) | collective-permute-done | bytes 98336 | tf_op jit(solution)/shard_map/ppermute | solution.py:32
  191.7 36.7 %all-reduce.264 = (f32[]{:T(128)}, f32[]{:T(128)}, f32[]{:T(128)}) all-reduce(f32[]{:T(128)} %get-tuple-element.86, f32[]{:T(128)S(6)} %mul.2741, f32[]{:T(128)S(6)} %mul.2737), channel_id=1, replica_groups=mesh['tm'=8,'lat'=4] {'tm','lat'}, use_global_device_ids=true, to_apply=%region_11.13 | all-reduce | flops 3 | bytes 24 | tf_op jit(solution)/shard_map/psum | solution.py:155
  229.1 4.5 %collective-permute-start.16 = (f32[3,8,2048]{2,1,0:T(8,128)S(1)}, f32[3,8,2048]{2,1,0:T(8,128)S(1)}, u32[]{:S(2)}, u32[]{:S(2)}) collective-permute-start(f32[3,8,2048]{2,1,0:T(8,128)S(1)} %multiply_subtract_fusion), channel_id=1, source_target_pairs={{4,0},{8,4},{12,8},{16,12},{20,16},{24,20},{28,24},{5,1},{9,5},{13... | collective-permute-start | bytes 589832 | tf_op jit(solution)/shard_map/ppermute | solution.py:42
  234.9 4.7 %collective-permute-start.14 = (f32[3,4,2048]{2,1,0:T(4,128)S(1)}, f32[3,4,2048]{2,1,0:T(4,128)S(1)}, u32[]{:S(2)}, u32[]{:S(2)}) collective-permute-start(f32[3,4,2048]{2,1,0:T(4,128)S(1)} %get-tuple-element.315), channel_id=1, source_target_pairs={{0,1},{1,2},{2,3},{4,5},{5,6},{6,7},{8,9},{9,10},{10,11},{12,13},{... | collective-permute-start | bytes 294920 | tf_op jit(solution)/shard_map/ppermute | solution.py:30
  239.7 1.9 collective-permute-start.15
  242.2 3.4 %collective-permute-done.15 = f32[3,4,2048]{2,1,0:T(4,128)S(1)} collective-permute-done((f32[3,4,2048]{2,1,0:T(4,128)S(1)}, f32[3,4,2048]{2,1,0:T(4,128)S(1)}, u32[]{:S(2)}, u32[]{:S(2)}) %collective-permute-start.15) | collective-permute-done | bytes 98336 | tf_op jit(solution)/shard_map/ppermute | solution.py:32
  (679 shorter events, 77.2 us)
Async XLA Ops:
  1.7 5.7 %copy-start.119 = (s32[2,128]{1,0:T(2,128)S(1)}, s32[2,128]{1,0:T(2,128)}, u32[]{:S(2)}) copy-start(s32[2,128]{1,0:T(2,128)} %param.21) | copy-start | bytes 3076
  1.7 15.1 %collective-permute-start = (f32[3,4,2048]{2,1,0:T(4,128)S(1)}, f32[3,4,2048]{2,1,0:T(4,128)S(1)}, u32[]{:S(2)}, u32[]{:S(2)}) collective-permute-start(f32[3,4,2048]{2,1,0:T(4,128)S(1)} %get-tuple-element.329), channel_id=1, source_target_pairs={{0,1},{1,2},{2,3},{4,5},{5,6},{6,7},{8,9},{9,10},{10,11},{12,13},{... | collective-permute-start | bytes 294920 | tf_op jit(solution)/shard_map/ppermute | solution.py:30
  5.4 11.4 %collective-permute-start.1 = (f32[3,4,2048]{2,1,0:T(4,128)S(1)}, f32[3,4,2048]{2,1,0:T(4,128)S(1)}, u32[]{:S(2)}, u32[]{:S(2)}) collective-permute-start(f32[3,4,2048]{2,1,0:T(4,128)S(1)} %get-tuple-element.330), channel_id=1, source_target_pairs={{1,0},{2,1},{3,2},{5,4},{6,5},{7,6},{9,8},{10,9},{11,10},{13,12},{... | collective-permute-start | bytes 294920 | tf_op jit(solution)/shard_map/ppermute | solution.py:32
  7.5 6.2 %copy-start.1 = (f32[1,3,8,2048]{3,2,1,0:T(8,128)S(1)}, f32[1,3,8,2048]{3,2,1,0:T(8,128)}, u32[]{:S(2)}) copy-start(f32[1,3,8,2048]{3,2,1,0:T(8,128)} %param.18) | copy-start | bytes 589828
  7.8 8.5 %collective-permute-start.2 = (f32[1,4,2048]{2,1,0:T(4,128)S(1)}, f32[1,4,2048]{2,1,0:T(4,128)S(1)}, u32[]{:S(2)}, u32[]{:S(2)}) collective-permute-start(f32[1,4,2048]{2,1,0:T(4,128)S(1)} %get-tuple-element.587), channel_id=1, source_target_pairs={{0,1},{1,2},{2,3},{4,5},{5,6},{6,7},{8,9},{9,10},{10,11},{12,13},{... | collective-permute-start | bytes 98312 | tf_op jit(solution)/shard_map/ppermute | solution.py:30
  11.4 5.2 %collective-permute-start.3 = (f32[1,4,2048]{2,1,0:T(4,128)S(1)}, f32[1,4,2048]{2,1,0:T(4,128)S(1)}, u32[]{:S(2)}, u32[]{:S(2)}) collective-permute-start(f32[1,4,2048]{2,1,0:T(4,128)S(1)} %get-tuple-element.588), channel_id=1, source_target_pairs={{1,0},{2,1},{3,2},{5,4},{6,5},{7,6},{9,8},{10,9},{11,10},{13,12},{... | collective-permute-start | bytes 98312 | tf_op jit(solution)/shard_map/ppermute | solution.py:32
  13.4 4.5 %copy-start.92 = (f32[14]{0:T(128)}, f32[14]{0:T(128)S(1)}, u32[]{:S(2)}) copy-start(f32[14]{0:T(128)S(1)} %get-tuple-element.603) | copy-start | bytes 172
  13.4 6.3 %copy-start.104 = (f32[14]{0:T(128)}, f32[14]{0:T(128)S(1)}, u32[]{:S(2)}) copy-start(f32[14]{0:T(128)S(1)} %get-tuple-element.604) | copy-start | bytes 172
  13.5 8.5 %copy-start.88 = (f32[12]{0:T(128)}, f32[12]{0:T(128)S(1)}, u32[]{:S(2)}) copy-start(f32[12]{0:T(128)S(1)} %get-tuple-element.601) | copy-start | bytes 148
  13.5 10.2 %copy-start.100 = (f32[12]{0:T(128)}, f32[12]{0:T(128)S(1)}, u32[]{:S(2)}) copy-start(f32[12]{0:T(128)S(1)} %get-tuple-element.602) | copy-start | bytes 148
  13.6 12.3 %copy-start.83 = (f32[10]{0:T(128)}, f32[10]{0:T(128)S(1)}, u32[]{:S(2)}) copy-start(f32[10]{0:T(128)S(1)} %get-tuple-element.599) | copy-start | bytes 124
  13.6 14.0 %copy-start.95 = (f32[10]{0:T(128)}, f32[10]{0:T(128)S(1)}, u32[]{:S(2)}) copy-start(f32[10]{0:T(128)S(1)} %get-tuple-element.600) | copy-start | bytes 124
  13.7 15.8 %copy-start.107 = (f32[8]{0:T(128)}, f32[8]{0:T(128)S(1)}, u32[]{:S(2)}) copy-start(f32[8]{0:T(128)S(1)} %get-tuple-element.598) | copy-start | bytes 100
  13.7 17.6 %copy-start.112 = (f32[8]{0:T(128)}, f32[8]{0:T(128)S(1)}, u32[]{:S(2)}) copy-start(f32[8]{0:T(128)S(1)} %get-tuple-element.597) | copy-start | bytes 100
  14.4 32.2 %copy-start.126 = (s32[128]{0:T(128)}, s32[128]{0:T(128)S(1)}, u32[]{:S(2)}) copy-start(s32[128]{0:T(128)S(1)} %compare_select_fusion) | copy-start | bytes 1540
  14.4 22.7 %copy-start.82 = (s32[1024]{0:T(1024)}, s32[1024]{0:T(1024)S(1)}, u32[]{:S(2)}) copy-start(s32[1024]{0:T(1024)S(1)} %pad_clamp_fusion) | copy-start | bytes 12292
  14.5 5.5 %copy-start.58 = (f32[14]{0:T(128)}, f32[14]{0:T(128)S(1)}, u32[]{:S(2)}) copy-start(f32[14]{0:T(128)S(1)} %slice.1569) | copy-start | bytes 172
  14.5 9.4 %copy-start.54 = (f32[12]{0:T(128)}, f32[12]{0:T(128)S(1)}, u32[]{:S(2)}) copy-start(f32[12]{0:T(128)S(1)} %slice.1602) | copy-start | bytes 148
  14.6 13.2 %copy-start.62 = (f32[10]{0:T(128)}, f32[10]{0:T(128)S(1)}, u32[]{:S(2)}) copy-start(f32[10]{0:T(128)S(1)} %slice.1635) | copy-start | bytes 124
  14.7 16.8 %copy-start.67 = (f32[8]{0:T(128)}, f32[8]{0:T(128)S(1)}, u32[]{:S(2)}) copy-start(f32[8]{0:T(128)S(1)} %slice.1667) | copy-start | bytes 100
  31.5 8.0 %collective-permute-start.4 = (f32[3,8,2048]{2,1,0:T(8,128)S(1)}, f32[3,8,2048]{2,1,0:T(8,128)S(1)}, u32[]{:S(2)}, u32[]{:S(2)}) collective-permute-start(f32[3,8,2048]{2,1,0:T(8,128)S(1)} %fusion.19), channel_id=1, source_target_pairs={{0,4},{4,8},{8,12},{12,16},{16,20},{20,24},{24,28},{1,5},{5,9},{9,... | collective-permute-start | bytes 589832 | tf_op jit(solution)/shard_map/ppermute | solution.py:42
  37.1 1.2 copy-start.117
  37.1 1.2 copy-start.122
  37.1 1.2 copy-start.127
  37.1 2.4 copy-start
  37.1 2.4 copy-start.3
  39.6 8.5 %collective-permute-start.5 = (f32[3,8,2048]{2,1,0:T(8,128)S(1)}, f32[3,8,2048]{2,1,0:T(8,128)S(1)}, u32[]{:S(2)}, u32[]{:S(2)}) collective-permute-start(f32[3,8,2048]{2,1,0:T(8,128)S(1)} %divide_select_fusion.1), channel_id=1, source_target_pairs={{4,0},{8,4},{12,8},{16,12},{20,16},{24,20},{28,24},{5,1},{9,5},{13... | collective-permute-start | bytes 589832 | tf_op jit(solution)/shard_map/ppermute | solution.py:42
  54.6 1.1 copy-start.24
  54.6 1.1 copy-start.52
  58.5 1.1 copy-start.16
  58.5 1.1 copy-start.44
  62.4 1.1 copy-start.7
  64.0 5.8 %collective-permute-start.6 = (f32[3,4,2048]{2,1,0:T(4,128)S(1)}, f32[3,4,2048]{2,1,0:T(4,128)S(1)}, u32[]{:S(2)}, u32[]{:S(2)}) collective-permute-start(f32[3,4,2048]{2,1,0:T(4,128)S(1)} %get-tuple-element.279), channel_id=1, source_target_pairs={{0,1},{1,2},{2,3},{4,5},{5,6},{6,7},{8,9},{9,10},{10,11},{12,13},{... | collective-permute-start | bytes 294920 | tf_op jit(solution)/shard_map/ppermute | solution.py:30
  67.8 5.9 %collective-permute-start.7 = (f32[3,4,2048]{2,1,0:T(4,128)S(1)}, f32[3,4,2048]{2,1,0:T(4,128)S(1)}, u32[]{:S(2)}, u32[]{:S(2)}) collective-permute-start(f32[3,4,2048]{2,1,0:T(4,128)S(1)} %get-tuple-element.278), channel_id=1, source_target_pairs={{1,0},{2,1},{3,2},{5,4},{6,5},{7,6},{9,8},{10,9},{11,10},{13,12},{... | collective-permute-start | bytes 294920 | tf_op jit(solution)/shard_map/ppermute | solution.py:32
  113.0 9.1 %collective-permute-start.8 = (f32[3,4,2048]{2,1,0:T(4,128)S(1)}, f32[3,4,2048]{2,1,0:T(4,128)S(1)}, u32[]{:S(2)}, u32[]{:S(2)}) collective-permute-start(f32[3,4,2048]{2,1,0:T(4,128)S(1)} %get-tuple-element.322), channel_id=1, source_target_pairs={{0,1},{1,2},{2,3},{4,5},{5,6},{6,7},{8,9},{9,10},{10,11},{12,13},{... | collective-permute-start | bytes 294920 | tf_op jit(solution)/shard_map/ppermute | solution.py:30
  118.3 5.9 %collective-permute-start.9 = (f32[3,4,2048]{2,1,0:T(4,128)S(1)}, f32[3,4,2048]{2,1,0:T(4,128)S(1)}, u32[]{:S(2)}, u32[]{:S(2)}) collective-permute-start(f32[3,4,2048]{2,1,0:T(4,128)S(1)} %get-tuple-element.323), channel_id=1, source_target_pairs={{1,0},{2,1},{3,2},{5,4},{6,5},{7,6},{9,8},{10,9},{11,10},{13,12},{... | collective-permute-start | bytes 294920 | tf_op jit(solution)/shard_map/ppermute | solution.py:32
  145.0 8.1 %collective-permute-start.10 = (f32[3,8,2048]{2,1,0:T(8,128)}, f32[3,8,2048]{2,1,0:T(8,128)}, u32[]{:S(2)}, u32[]{:S(2)}) collective-permute-start(f32[3,8,2048]{2,1,0:T(8,128)} %fusion.18), channel_id=1, source_target_pairs={{0,4},{4,8},{8,12},{12,16},{16,20},{20,24},{24,28},{1,5},{5,9},{9,... | collective-permute-start | bytes 589832 | tf_op jit(solution)/shard_map/ppermute | solution.py:42
  149.2 2.6 %copy-start.124 = (f32[1,128]{1,0:T(1,128)S(1)}, f32[1,128]{1,0:T(1,128)}, u32[]{:S(2)}) copy-start(f32[1,128]{1,0:T(1,128)} %get-tuple-element.92) | copy-start | bytes 1540
  150.5 1.3 copy-start.125
  154.1 9.9 %collective-permute-start.11 = (f32[3,8,2048]{2,1,0:T(8,128)S(1)}, f32[3,8,2048]{2,1,0:T(8,128)S(1)}, u32[]{:S(2)}, u32[]{:S(2)}) collective-permute-start(f32[3,8,2048]{2,1,0:T(8,128)S(1)} %divide_select_fusion), channel_id=1, source_target_pairs={{4,0},{8,4},{12,8},{16,12},{20,16},{24,20},{28,24},{5,1},{9,5},{13... | collective-permute-start | bytes 589832 | tf_op jit(solution)/shard_map/ppermute | solution.py:42
  169.9 1.1 copy-start.22
  173.8 1.1 copy-start.14
  179.9 5.7 %collective-permute-start.12 = (f32[3,4,2048]{2,1,0:T(4,128)S(1)}, f32[3,4,2048]{2,1,0:T(4,128)S(1)}, u32[]{:S(2)}, u32[]{:S(2)}) collective-permute-start(f32[3,4,2048]{2,1,0:T(4,128)S(1)} %get-tuple-element.242), channel_id=1, source_target_pairs={{0,1},{1,2},{2,3},{4,5},{5,6},{6,7},{8,9},{9,10},{10,11},{12,13},{... | collective-permute-start | bytes 294920 | tf_op jit(solution)/shard_map/ppermute | solution.py:30
  183.7 5.9 %collective-permute-start.13 = (f32[3,4,2048]{2,1,0:T(4,128)S(1)}, f32[3,4,2048]{2,1,0:T(4,128)S(1)}, u32[]{:S(2)}, u32[]{:S(2)}) collective-permute-start(f32[3,4,2048]{2,1,0:T(4,128)S(1)} %get-tuple-element.241), channel_id=1, source_target_pairs={{1,0},{2,1},{3,2},{5,4},{6,5},{7,6},{9,8},{10,9},{11,10},{13,12},{... | collective-permute-start | bytes 294920 | tf_op jit(solution)/shard_map/ppermute | solution.py:32
  229.1 16.5 %copy-start.2 = (f32[3,8,2048]{2,1,0:T(8,128)}, f32[3,8,2048]{2,1,0:T(8,128)S(1)}, u32[]{:S(2)}) copy-start(f32[3,8,2048]{2,1,0:T(8,128)S(1)} %multiply_subtract_fusion) | copy-start | bytes 589828
  229.1 24.7 %collective-permute-start.16 = (f32[3,8,2048]{2,1,0:T(8,128)S(1)}, f32[3,8,2048]{2,1,0:T(8,128)S(1)}, u32[]{:S(2)}, u32[]{:S(2)}) collective-permute-start(f32[3,8,2048]{2,1,0:T(8,128)S(1)} %multiply_subtract_fusion), channel_id=1, source_target_pairs={{4,0},{8,4},{12,8},{16,12},{20,16},{24,20},{28,24},{5,1},{9,5},{13... | collective-permute-start | bytes 589832 | tf_op jit(solution)/shard_map/ppermute | solution.py:42
  234.9 7.3 %collective-permute-start.14 = (f32[3,4,2048]{2,1,0:T(4,128)S(1)}, f32[3,4,2048]{2,1,0:T(4,128)S(1)}, u32[]{:S(2)}, u32[]{:S(2)}) collective-permute-start(f32[3,4,2048]{2,1,0:T(4,128)S(1)} %get-tuple-element.315), channel_id=1, source_target_pairs={{0,1},{1,2},{2,3},{4,5},{5,6},{6,7},{8,9},{9,10},{10,11},{12,13},{... | collective-permute-start | bytes 294920 | tf_op jit(solution)/shard_map/ppermute | solution.py:30
  239.7 5.9 %collective-permute-start.15 = (f32[3,4,2048]{2,1,0:T(4,128)S(1)}, f32[3,4,2048]{2,1,0:T(4,128)S(1)}, u32[]{:S(2)}, u32[]{:S(2)}) collective-permute-start(f32[3,4,2048]{2,1,0:T(4,128)S(1)} %get-tuple-element.316), channel_id=1, source_target_pairs={{1,0},{2,1},{3,2},{5,4},{6,5},{7,6},{9,8},{10,9},{11,10},{13,12},{... | collective-permute-start | bytes 294920 | tf_op jit(solution)/shard_map/ppermute | solution.py:32
  (97 other events, 78.2 us)
where the time goes:
time: 257 us; the launch traced here: 255 us
  local copies, waits for them, and re-layouts  74.5 us (29%)
  blocking collectives  74.3 us (29%)
  starting transfers between devices  51.9 us (20%)
  other arithmetic  31.4 us (12%)
  waiting for transfers between devices  13.9 us (5%)
  between operations  9.19 us (4%)
    psum x2, blocking collectives, shards(): steepness = lax.psum(local_steep, ('tm', 'lat'))  74.3 us
    unnamed x270, local copies, waits for them, and re-layouts  29.7 us
    ppermute x6, starting transfers between devices, extended_2(): lax.ppermute(tail, axis, [(i, (i + 1) % count) for i in range(ends)])  23.6 us
    slice x56, local copies, waits for them, and re-layouts, zonal_diff(): return 0.5 * (jnp.roll(field, -1, axis=1) - jnp.roll(field, 1, axis=1))  22.9 us
    ppermute x5, starting transfers between devices, passed_along(): return lax.ppermute(x, axis, pairs)  16.8 us
    ppermute x6, waiting for transfers between devices, extended_2(): lax.ppermute(head, axis, [((i + 1) % count, i) for i in range(ends)])  13.8 us
    ppermute x6, starting transfers between devices, extended_2(): lax.ppermute(head, axis, [((i + 1) % count, i) for i in range(ends)])  11.5 us
    scatter-add x8, other arithmetic, deep_run(): values = jnp.take(inner[0].reshape(-1), cell_ids)  11.1 us
  transfers between devices with their start and end apart: 17, of which 5 were waited for; matrix products, arithmetic and copies ran while one was open for 12% of the time, Pallas kernels for 0%

commit v1 on v0

v1 whole, which is shorter than its diff:
```python
import functools

import jax
import jax.numpy as jnp
from jax import lax
from jax.experimental import pallas as pl
from jax.experimental.pallas import tpu as pltpu
from jax.sharding import PartitionSpec as P

STEPS = 4
ITERS = 2
TILE_LAT = 4
TILE_LON = 16

TIME_STEP = 0.25
MEAN_DEPTH = 1.0
DRAG_RATE = 0.02
STEP_LENGTH = 0.3
CORIOLIS_MEAN = 0.3
CORIOLIS_SLOPE = 0.2
EPSILON = 1e-06

MESH = pl.DeviceIdType.MESH
LANES = 128
WIDTH = 512
DIRECT_MAX = 64


def split3(x):
    hi = x.astype(jnp.bfloat16)
    rest = x - hi.astype(jnp.float32)
    mid = rest.astype(jnp.bfloat16)
    low = (rest - mid.astype(jnp.float32)).astype(jnp.bfloat16)
    return jnp.concatenate([hi, mid, low], axis=0)


def join3(y):
    n = y.shape[0] // 3
    return (y[2 * n :] + y[n : 2 * n]) + y[:n]


def fold_lanes(x):
    total = x[:, :LANES]
    for c in range(LANES, x.shape[1], LANES):
        total = total + x[:, c : c + LANES]
    return jnp.sum(total, axis=0, keepdims=True)


def kernel(
    n_tm, n_lat,
    states, background, error_std, land_mask, obs_cells, obs_moments, obs_values, obs_error,
    est_out, slid_out, costs_out,
    xs, deriv, lam, forcing, onehot, gain, cor, masks, variance, inv_var,
    xnext, fe_prev, adj_in, dir_buf, dir_halo, dir_next, parts, parts_tm,
    ssem, rsem,
):
    tm = lax.axis_index("tm")
    lat = lax.axis_index("lat")
    rows = background.shape[1]
    lon = background.shape[2]
    wide = 2 * rows
    half = STEPS
    width = min(WIDTH, lon)
    tiles = lon // width
    total_rows = rows * n_lat
    cell_count = 3 * total_rows * lon
    n_dev = n_tm * n_lat
    me = tm * n_lat + lat
    has_up = lat > 0
    has_down = lat < n_lat - 1
    has_prev = tm > 0
    has_next = tm < n_tm - 1
    up = {"lat": lat - 1}
    down = {"lat": lat + 1}
    before = {"tm": tm - 1}
    after = {"tm": tm + 1}
    direct = n_dev <= DIRECT_MAX

    def all_partner(d):
        rank = (me + d) % n_dev
        return {"tm": rank // n_lat, "lat": rank % n_lat}

    def lat_partner(d):
        return {"lat": (lat + d) % n_lat}

    def tm_partner(d):
        return {"tm": (tm + d) % n_tm}

    barrier = pltpu.get_barrier_semaphore()
    if direct:
        partners = [all_partner(d) for d in range(1, n_dev)]
    else:
        partners = [lat_partner(d) for d in range(1, n_lat)]
        partners += [tm_partner(d) for d in range(1, n_tm)]
    for partner in partners:
        pl.semaphore_signal(barrier, inc=1, device_id=partner, device_id_type=MESH)

    def remote(src, dst, k, device):
        return pltpu.make_async_remote_copy(
            src_ref=src, dst_ref=dst, send_sem=ssem.at[k], recv_sem=rsem.at[k],
            device_id=device, device_id_type=MESH,
        )

    pending = []

    def send(cond, src, dst, k, device):
        @pl.when(cond)
        def _():
            remote(src, dst, k, device).start()

        pending.append((cond, src, k, device))

    def drain():
        for cond, src, k, device in pending:
            @pl.when(cond)
            def _(src=src, k=k, device=device):
                remote(src, src, k, device).wait_send()
        pending.clear()

    def arrive(cond, dst, k, device):
        @pl.when(cond)
        def _():
            remote(dst, dst, k, device).wait_recv()

    zeros_half = jnp.zeros((3, half, lon), jnp.float32)
    lo, hi = slice(0, half), slice(half, rows)
    lo_w, hi_w = slice(rows, rows + half), slice(rows + half, wide)
    own = slice(0, rows)

    @pl.when(lat == n_lat - 1)
    def _():
        xs[0, :, lo_w, :] = zeros_half
        masks[lo_w, :] = jnp.zeros((half, LANES), jnp.float32)
        for it in range(ITERS):
            adj_in[it, :, hi, :] = zeros_half
            dir_halo[it, :, lo, :] = zeros_half

    @pl.when(lat == 0)
    def _():
        xs[0, :, hi_w, :] = zeros_half
        masks[hi_w, :] = jnp.zeros((half, LANES), jnp.float32)
        for it in range(ITERS):
            adj_in[it, :, lo, :] = zeros_half
            dir_halo[it, :, hi, :] = zeros_half

    @pl.when(tm == n_tm - 1)
    def _():
        xnext[...] = jnp.zeros(xnext.shape, jnp.float32)
        for it in range(ITERS):
            dir_next[it] = jnp.zeros(xnext.shape, jnp.float32)

    @pl.when(tm == 0)
    def _():
        for it in range(ITERS):
            fe_prev[it] = background[...]

    mask = land_mask[...].astype(jnp.float32)
    tile_cols = mask.shape[1]
    masks[own, :] = jnp.concatenate(
        [jnp.broadcast_to(mask[i : i + 1], (TILE_LAT, tile_cols)) for i in range(rows // TILE_LAT)],
        axis=0,
    )

    pl.semaphore_wait(barrier, len(partners))

    send(has_up, masks.at[lo], masks.at[lo_w], 0, up)
    send(has_down, masks.at[hi], masks.at[hi_w], 1, down)
    send(has_up, states.at[0, :, lo], xs.at[0, :, lo_w], 2, up)
    send(has_down, states.at[0, :, hi], xs.at[0, :, hi_w], 3, down)
    send(has_prev, states.at[0], xnext, 4, before)

    xs[0, :, own, :] = states[0]
    var = error_std[...] * error_std[...]
    variance[...] = var
    inv_var[...] = 1.0 / var
    cells = obs_cells[...]
    n_obs = cells.shape[1]
    cell_row = jnp.zeros_like(cells)
    for r in range(1, rows):
        cell_row = cell_row + (cells >= r * lon).astype(jnp.int32)
    cell_col = cells - cell_row * lon
    onehot[...] = (
        lax.broadcasted_iota(jnp.int32, (lon, n_obs), 0) == cell_col
    ).astype(jnp.float32).astype(jnp.bfloat16)
    taken = (
        lax.broadcasted_iota(jnp.int32, (STEPS * rows, n_obs), 0)
        == obs_moments[...] * rows + cell_row
    ).astype(jnp.float32)
    targets = obs_values[...]
    precision = 1.0 / (obs_error[...] * obs_error[...])
    r_id = lax.broadcasted_iota(jnp.int32, (wide, LANES), 0)
    r_id = jnp.where(r_id < rows + half, r_id, r_id - wide) + lat * rows
    cor[...] = CORIOLIS_MEAN + CORIOLIS_SLOPE * (r_id.astype(jnp.float32) / total_rows - 0.5)
    lam[STEPS, :, rows:wide, :] = jnp.zeros((3, rows, lon), jnp.float32)

    arrive(has_down, masks.at[lo_w], 0, down)
    arrive(has_up, masks.at[hi_w], 1, up)
    first_col = lax.broadcasted_iota(jnp.int32, (tile_cols, lon), 0) * TILE_LON
    col = lax.broadcasted_iota(jnp.int32, (tile_cols, lon), 1)
    grow = ((col >= first_col) & (col < first_col + TILE_LON)).astype(jnp.float32)
    gain[...] = TIME_STEP * jnp.dot(
        masks[...].astype(jnp.bfloat16), grow.astype(jnp.bfloat16),
        preferred_element_type=jnp.float32,
    )
    arrive(has_down, xs.at[0, :, lo_w], 2, down)
    arrive(has_up, xs.at[0, :, hi_w], 3, up)

    def ext(ref, index, j):
        c = j * width
        left = (c - LANES) % lon
        right = (c + width) % lon
        return jnp.concatenate(
            [
                ref[index + (slice(None), slice(left, left + LANES))],
                ref[index + (slice(None), slice(c, c + width))],
                ref[index + (slice(None), slice(right, right + LANES))],
            ],
            axis=-1,
        )

    def mid(e):
        return e[:, LANES : LANES + width]

    def dx2(e):
        return mid(pltpu.roll(e, width + 2 * LANES - 1, 1)) - mid(pltpu.roll(e, 1, 1))

    def east(e):
        return mid(pltpu.roll(e, width + 2 * LANES - 1, 1))

    def west(e):
        return mid(pltpu.roll(e, 1, 1))

    def north(a):
        return pltpu.roll(a, wide - 1, 0)

    def south(a):
        return pltpu.roll(a, 1, 0)

    def dy2(a):
        return north(a) - south(a)

    def coriolis():
        return jnp.concatenate([cor[...]] * (width // LANES), axis=-1)

    def forward_step(s, carry):
        for j in range(tiles):
            span = slice(j * width, (j + 1) * width)
            he, ue, ve = (ext(xs, (s, f), j) for f in range(3))
            h, u, v = mid(he), mid(ue), mid(ve)
            h_e, h_w, u_e, u_w = east(he), west(he), east(ue), west(ue)
            h_n, h_s, v_n, v_s = north(h), south(h), north(v), south(v)
            ux = 0.5 * (u_e - u_w)
            vx = 0.5 * dx2(ve)
            uy = 0.5 * dy2(u)
            vy = 0.5 * (v_n - v_s)
            g = gain[:, span]
            f = coriolis()
            dh = -0.5 * (
                ((MEAN_DEPTH + h_e) * u_e - (MEAN_DEPTH + h_w) * u_w)
                + ((MEAN_DEPTH + h_n) * v_n - (MEAN_DEPTH + h_s) * v_s)
            )
            du = f * v - 0.5 * (h_e - h_w) - u * ux - v * uy - DRAG_RATE * u
            dv = -f * u - 0.5 * (h_n - h_s) - u * vx - v * vy - DRAG_RATE * v
            xs[s + 1, 0, :, span] = h + g * dh
            xs[s + 1, 1, :, span] = u + g * du
            xs[s + 1, 2, :, span] = v + g * dv
            deriv[s, 0, :, span] = ux
            deriv[s, 1, :, span] = uy
            deriv[s, 2, :, span] = vx
            deriv[s, 3, :, span] = vy
        return carry

    def adjoint_step(i, carry):
        s = STEPS - 1 - i
        for j in range(tiles):
            span = slice(j * width, (j + 1) * width)
            ge = ext(gain, (), j)
            lh, lu, lv = (ext(lam, (s + 1, f), j) for f in range(3))
            ae, be, ce = lh * ge, lu * ge, lv * ge
            ue = ext(xs, (s, 1), j)
            a, b, c, u = mid(ae), mid(be), mid(ce), mid(ue)
            v = xs[s, 2, :, span]
            depth = 0.5 * (MEAN_DEPTH + xs[s, 0, :, span])
            f = coriolis()
            ax, ay = dx2(ae), dy2(a)
            obs = jnp.concatenate(
                [forcing[s, :, span], jnp.zeros((rows, width), jnp.float32)], axis=0
            )
            lam[s, 0, :, span] = (
                mid(lh) + obs + 0.5 * (u * ax + v * ay + dx2(be) + dy2(c))
            )
            lam[s, 1, :, span] = (
                mid(lu)
                + depth * ax
                + 0.5 * (dx2(ue * be) + dy2(v * b))
                - b * (deriv[s, 0, :, span] + DRAG_RATE)
                - c * (f + deriv[s, 2, :, span])
            )
            lam[s, 2, :, span] = (
                mid(lv)
                + depth * ay
                + 0.5 * (dx2(ue * ce) + dy2(v * c))
                + b * (f - deriv[s, 1, :, span])
                - c * (deriv[s, 3, :, span] + DRAG_RATE)
            )
        return carry

    def exchange(buf, value, k, size, mine, partner):
        buf[mine] = value
        for d in range(1, size):
            remote(buf.at[mine], buf.at[mine], k, partner(d)).start()

    def collect(buf, k, size, partner):
        remote(buf.at[0 : size - 1], buf.at[0 : size - 1], k, partner(1)).wait_recv()
        total = jnp.sum(buf[...], axis=0)
        return total

    def sent(buf, k, size, partner):
        remote(buf.at[0 : size - 1], buf.at[0 : size - 1], k, partner(1)).wait_send()

    scale = None
    for it in range(ITERS):
        base = 5 + 8 * it
        lax.fori_loop(0, STEPS, forward_step, 0)
        send(has_next, xs.at[STEPS, :, own], fe_prev.at[it], base, after)

        heights = jnp.concatenate([xs[s, 0, own, :] for s in range(STEPS)], axis=0)
        seen = join3(
            jnp.dot(split3(heights), onehot[...], preferred_element_type=jnp.float32)
        )
        misfit = jnp.sum(seen * taken, axis=0, keepdims=True) - targets
        weighted = misfit * precision
        spread = join3(
            lax.dot_general(
                split3(taken * weighted), onehot[...], (((1,), (1,)), ((), ())),
                preferred_element_type=jnp.float32,
            )
        )
        for s in range(STEPS):
            forcing[s] = spread[s * rows : (s + 1) * rows]

        if it == 0:
            arrive(has_next, xnext, 4, after)
        else:
            arrive(has_next, dir_next.at[it - 1], base - 8 + 5, after)
            xnext[...] = xnext[...] - scale * dir_next[it - 1]

        @pl.when(has_next)
        def _():
            lam[STEPS, :, own, :] = (xs[STEPS, :, own, :] - xnext[...]) * inv_var[...]

        @pl.when(tm == n_tm - 1)
        def _():
            lam[STEPS, :, own, :] = jnp.zeros((3, rows, lon), jnp.float32)

        lax.fori_loop(0, STEPS, adjoint_step, 0)
        send(has_down, lam.at[0, :, lo_w], adj_in.at[it, :, lo], base + 1, down)
        send(has_up, lam.at[0, :, hi_w], adj_in.at[it, :, hi], base + 2, up)

        arrive(has_prev, fe_prev.at[it], base, before)
        cost = misfit * weighted
        for f in range(3):
            gap = xs[0, f, own, :] - fe_prev[it, f]
            cost = cost + fold_lanes(gap * gap * inv_var[f])
            dir_buf[it, f] = gap + variance[f] * lam[0, f, own, :]
        arrive(has_up, adj_in.at[it, :, lo], base + 1, up)
        arrive(has_down, adj_in.at[it, :, hi], base + 2, down)
        steep = jnp.zeros((1, LANES), jnp.float32)
        for f in range(3):
            direction = dir_buf[it, f] + variance[f] * adj_in[it, f]
            dir_buf[it, f] = direction
            steep = steep + fold_lanes(direction * direction * inv_var[f])

        message = jnp.concatenate([steep, cost], axis=0)
        if direct:
            exchange(parts.at[it], message, base + 6, n_dev, me, all_partner)
        else:
            exchange(parts.at[it], message, base + 6, n_lat, lat, lat_partner)
        send(has_up, dir_buf.at[it, :, lo], dir_halo.at[it, :, lo], base + 3, up)
        send(has_down, dir_buf.at[it, :, hi], dir_halo.at[it, :, hi], base + 4, down)
        if direct:
            send(has_prev, dir_buf.at[it], dir_next.at[it], base + 5, before)
            total = collect(parts.at[it], base + 6, n_dev, all_partner)
        else:
            total = collect(parts.at[it], base + 6, n_lat, lat_partner)
            exchange(parts_tm.at[it], total, base + 7, n_tm, tm, tm_partner)
            send(has_prev, dir_buf.at[it], dir_next.at[it], base + 5, before)
            total = collect(parts_tm.at[it], base + 7, n_tm, tm_partner)
        steepness = jnp.sum(total[0:1], axis=1, keepdims=True)
        scale = STEP_LENGTH / jnp.sqrt(steepness / (n_tm * cell_count) + EPSILON)
        costs_out[it] = jnp.sum(total[1:2]) * (0.5 / cell_count)

        for f in range(3):
            xs[0, f, own, :] = xs[0, f, own, :] - scale * dir_buf[it, f]
        arrive(has_down, dir_halo.at[it, :, lo], base + 3, down)
        arrive(has_up, dir_halo.at[it, :, hi], base + 4, up)
        for f in range(3):
            xs[0, f, rows:wide, :] = xs[0, f, rows:wide, :] - scale * dir_halo[it, f]
        drain()
        if direct:
            sent(parts.at[it], base + 6, n_dev, all_partner)
        else:
            sent(parts.at[it], base + 6, n_lat, lat_partner)
            sent(parts_tm.at[it], base + 7, n_tm, tm_partner)

    est_out[0] = xs[0, :, own, :]
    lax.fori_loop(0, STEPS, forward_step, 0)
    arrive(has_next, dir_next.at[ITERS - 1], 5 + 8 * (ITERS - 1) + 5, after)

    @pl.when(has_next)
    def _():
        slid_out[0] = xnext[...] - scale * dir_next[ITERS - 1]

    @pl.when(tm == n_tm - 1)
    def _():
        slid_out[0] = xs[STEPS, :, own, :]


def shards(n_tm, n_lat, *args):
    states, background = args[0], args[1]
    _, rows, lon = background.shape
    n_obs = args[4].shape[1]
    wide = 2 * rows
    f32 = jnp.float32
    direct = n_tm * n_lat <= DIRECT_MAX
    field = (3, rows, lon)
    sems = 5 + 8 * ITERS
    return pl.pallas_call(
        functools.partial(kernel, n_tm, n_lat),
        out_shape=(
            jax.ShapeDtypeStruct(states.shape, f32),
            jax.ShapeDtypeStruct(states.shape, f32),
            jax.ShapeDtypeStruct((ITERS,), f32),
        ),
        in_specs=[pl.BlockSpec(memory_space=pltpu.VMEM)] * 8,
        out_specs=(
            pl.BlockSpec(memory_space=pltpu.VMEM),
            pl.BlockSpec(memory_space=pltpu.VMEM),
            pl.BlockSpec(memory_space=pltpu.SMEM),
        ),
        scratch_shapes=[
            pltpu.VMEM((STEPS + 1, 3, wide, lon), f32),
            pltpu.VMEM((STEPS, 4, wide, lon), f32),
            pltpu.VMEM((STEPS + 1, 3, wide, lon), f32),
            pltpu.VMEM((STEPS, rows, lon), f32),
            pltpu.VMEM((lon, n_obs), jnp.bfloat16),
            pltpu.VMEM((wide, lon), f32),
            pltpu.VMEM((wide, LANES), f32),
            pltpu.VMEM((wide, LANES), f32),
            pltpu.VMEM(field, f32),
            pltpu.VMEM(field, f32),
            pltpu.VMEM(field, f32),
            pltpu.VMEM((ITERS,) + field, f32),
            pltpu.VMEM((ITERS,) + field, f32),
            pltpu.VMEM((ITERS,) + field, f32),
            pltpu.VMEM((ITERS,) + field, f32),
            pltpu.VMEM((ITERS,) + field, f32),
            pltpu.VMEM((ITERS, n_tm * n_lat if direct else n_lat, 2, LANES), f32),
            pltpu.VMEM((ITERS, n_tm, 2, LANES), f32),
            pltpu.SemaphoreType.DMA((sems,)),
            pltpu.SemaphoreType.DMA((sems,)),
        ],
        compiler_params=pltpu.CompilerParams(
            collective_id=0, has_side_effects=True, vmem_limit_bytes=40 * 1024 * 1024
        ),
    )(*args)


def solution(mesh):
    placed = (
        P("tm", None, "lat", None),
        P(None, "lat", None),
        P(None, "lat", None),
        P("lat", None),
        P("tm", "lat"),
        P("tm", "lat"),
        P("tm", "lat"),
        P("tm", "lat"),
    )
    return jax.shard_map(
        functools.partial(shards, mesh.shape["tm"], mesh.shape["lat"]),
        mesh=mesh,
        in_specs=placed,
        out_specs=(P("tm", None, "lat", None), P("tm", None, "lat", None), P()),
        check_vma=False,
    )
```

time: 257 us -> 48.4 us (0.19)
  the two profiles are of different devices: /device:TPU:9 before, /device:TPU:0 now
where the time goes in v1:
time: 48.4 us; the launch traced here: 48.1 us
  Pallas kernels  39.5 us (82%)
  local copies, waits for them, and re-layouts  7.94 us (16%)
  between operations  0.66 us (1%)
    pallas_call x1, Pallas kernels, shards(): pl.pallas_call(functools.partial(kernel, n_tm, n_lat), out_shape=(jax.Sha...  39.5 us
    unnamed x19, local copies, waits for them, and re-layouts  7.94 us

profile of v1, /device:TPU:0, one launch (start us, length us, event | category | flops | bytes accessed | tf_op | source)
XLA Modules:
  0.0 48.1 jit_solution(15190469269579084954)
XLA Ops:
  0.6 0.0 copy-start
  0.6 0.9 %copy-done = f32[1,3,8,2048]{3,2,1,0:T(8,128)S(1)} copy-done((f32[1,3,8,2048]{3,2,1,0:T(8,128)S(1)}, f32[1,3,8,2048]{3,2,1,0:T(8,128)}, u32[]{:S(2)}) %copy-start) | copy-done | bytes 196632
  1.6 0.0 copy-start.1
  1.6 0.9 %copy-done.1 = f32[3,8,2048]{2,1,0:T(8,128)S(1)} copy-done((f32[3,8,2048]{2,1,0:T(8,128)S(1)}, f32[3,8,2048]{2,1,0:T(8,128)}, u32[]{:S(2)}) %copy-start.1) | copy-done | bytes 196632
  2.5 0.0 copy-start.2
  2.5 0.9 %copy-done.2 = f32[3,8,2048]{2,1,0:T(8,128)S(1)} copy-done((f32[3,8,2048]{2,1,0:T(8,128)S(1)}, f32[3,8,2048]{2,1,0:T(8,128)}, u32[]{:S(2)}) %copy-start.2) | copy-done | bytes 196632
  3.4 0.0 copy-start.3
  3.4 0.7 %copy-done.3 = s32[2,128]{1,0:T(2,128)S(1)} copy-done((s32[2,128]{1,0:T(2,128)S(1)}, s32[2,128]{1,0:T(2,128)}, u32[]{:S(2)}) %copy-start.3) | copy-done | bytes 1048
  4.1 0.0 copy-start.4
  4.1 0.7 %copy-done.4 = s32[1,128]{1,0:T(1,128)S(1)} copy-done((s32[1,128]{1,0:T(1,128)S(1)}, s32[1,128]{1,0:T(1,128)}, u32[]{:S(2)}) %copy-start.4) | copy-done | bytes 536
  4.8 0.0 copy-start.5
  4.8 0.7 %copy-done.5 = s32[1,128]{1,0:T(1,128)S(1)} copy-done((s32[1,128]{1,0:T(1,128)S(1)}, s32[1,128]{1,0:T(1,128)}, u32[]{:S(2)}) %copy-start.5) | copy-done | bytes 536
  5.4 0.0 copy-start.6
  5.4 0.7 %copy-done.6 = f32[1,128]{1,0:T(1,128)S(1)} copy-done((f32[1,128]{1,0:T(1,128)S(1)}, f32[1,128]{1,0:T(1,128)}, u32[]{:S(2)}) %copy-start.6) | copy-done | bytes 536
  6.1 0.0 copy-start.7
  6.1 0.7 %copy-done.7 = f32[1,128]{1,0:T(1,128)S(1)} copy-done((f32[1,128]{1,0:T(1,128)S(1)}, f32[1,128]{1,0:T(1,128)}, u32[]{:S(2)}) %copy-start.7) | copy-done | bytes 536
  6.7 39.5 %shard_map.103 = (f32[1,3,8,2048]{3,2,1,0:T(8,128)S(1)}, f32[1,3,8,2048]{3,2,1,0:T(8,128)S(1)}, f32[2]{0:T(128)S(1)}) custom-call(f32[1,3,8,2048]{3,2,1,0:T(8,128)S(1)} %copy-done, f32[3,8,2048]{2,1,0:T(8,128)S(1)} %copy-done.1, f32[3,8,2048]{2,1,0:T(8,128)S(1)} %copy-done.2, s32[2,128]{1,0:T(2,128)S(1)} %copy-done.3, s32[1,128]{1,0:T(1,128)S(1)} %copy-done.4, ...), custom_call_target="tpu_custom_call" | custom-call | tf_op jit(solution)/shard_map/pallas_call | solution.py:428
  46.2 0.7 %copy.14 = f32[1,3,8,2048]{3,2,1,0:T(8,128)} copy(f32[1,3,8,2048]{3,2,1,0:T(8,128)S(1)} %get-tuple-element.6) | data formatting | bytes 393216
  46.9 0.7 %copy.15 = f32[1,3,8,2048]{3,2,1,0:T(8,128)} copy(f32[1,3,8,2048]{3,2,1,0:T(8,128)S(1)} %get-tuple-element.7) | data formatting | bytes 393216
  47.6 0.5 %copy.16 = f32[2]{0:T(128)} copy(f32[2]{0:T(128)S(1)} %get-tuple-element.8) | data formatting | bytes 16
Async XLA Ops:
  0.6 0.9 %copy-start = (f32[1,3,8,2048]{3,2,1,0:T(8,128)S(1)}, f32[1,3,8,2048]{3,2,1,0:T(8,128)}, u32[]{:S(2)}) copy-start(f32[1,3,8,2048]{3,2,1,0:T(8,128)} %states.1) | copy-start | bytes 589828
  1.6 0.9 %copy-start.1 = (f32[3,8,2048]{2,1,0:T(8,128)S(1)}, f32[3,8,2048]{2,1,0:T(8,128)}, u32[]{:S(2)}) copy-start(f32[3,8,2048]{2,1,0:T(8,128)} %background.1) | copy-start | bytes 589828
  2.5 0.9 %copy-start.2 = (f32[3,8,2048]{2,1,0:T(8,128)S(1)}, f32[3,8,2048]{2,1,0:T(8,128)}, u32[]{:S(2)}) copy-start(f32[3,8,2048]{2,1,0:T(8,128)} %error_std.1) | copy-start | bytes 589828
  3.4 0.7 %copy-start.3 = (s32[2,128]{1,0:T(2,128)S(1)}, s32[2,128]{1,0:T(2,128)}, u32[]{:S(2)}) copy-start(s32[2,128]{1,0:T(2,128)} %land_mask.1) | copy-start | bytes 3076
  4.1 0.7 %copy-start.4 = (s32[1,128]{1,0:T(1,128)S(1)}, s32[1,128]{1,0:T(1,128)}, u32[]{:S(2)}) copy-start(s32[1,128]{1,0:T(1,128)} %obs_cells.1) | copy-start | bytes 1540
  4.8 0.7 %copy-start.5 = (s32[1,128]{1,0:T(1,128)S(1)}, s32[1,128]{1,0:T(1,128)}, u32[]{:S(2)}) copy-start(s32[1,128]{1,0:T(1,128)} %obs_moments.1) | copy-start | bytes 1540
  5.4 0.7 %copy-start.6 = (f32[1,128]{1,0:T(1,128)S(1)}, f32[1,128]{1,0:T(1,128)}, u32[]{:S(2)}) copy-start(f32[1,128]{1,0:T(1,128)} %obs_values.1) | copy-start | bytes 1540
  6.1 0.7 %copy-start.7 = (f32[1,128]{1,0:T(1,128)S(1)}, f32[1,128]{1,0:T(1,128)}, u32[]{:S(2)}) copy-start(f32[1,128]{1,0:T(1,128)} %obs_error.1) | copy-start | bytes 1540

commit v2 on v1

--- a/solution.py
+++ b/solution.py
@@ -48,16 +48,17 @@
 
 def kernel(
     n_tm, n_lat,
-    states, background, error_std, land_mask, obs_cells, obs_moments, obs_values, obs_error,
+    states_hbm, background_hbm, error_hbm, mask_hbm, cells_hbm, moments_hbm, values_hbm, obs_err_hbm,
     est_out, slid_out, costs_out,
     xs, deriv, lam, forcing, onehot, gain, cor, masks, variance, inv_var,
     xnext, fe_prev, adj_in, dir_buf, dir_halo, dir_next, parts, parts_tm,
-    ssem, rsem,
+    error_std, land_mask, obs_cells, obs_moments, obs_values, obs_error,
+    ssem, rsem, lsem,
 ):
     tm = lax.axis_index("tm")
     lat = lax.axis_index("lat")
-    rows = background.shape[1]
-    lon = background.shape[2]
+    rows = variance.shape[1]
+    lon = variance.shape[2]
     wide = 2 * rows
     half = STEPS
     width = min(WIDTH, lon)
@@ -76,24 +77,44 @@
     after = {"tm": tm + 1}
     direct = n_dev <= DIRECT_MAX
 
-    def all_partner(d):
-        rank = (me + d) % n_dev
-        return {"tm": rank // n_lat, "lat": rank % n_lat}
-
-    def lat_partner(d):
-        return {"lat": (lat + d) % n_lat}
-
-    def tm_partner(d):
-        return {"tm": (tm + d) % n_tm}
-
+    def wrapped(i, n):
+        return jnp.where(i >= n, i - n, i)
+
+    lats = [lat] + [wrapped(lat + d, n_lat) for d in range(1, n_lat)]
+    tms = [tm] + [wrapped(tm + d, n_tm) for d in range(1, n_tm)]
+    lat_partners = [{"lat": lats[d]} for d in range(1, n_lat)]
+    tm_partners = [{"tm": tms[d]} for d in range(1, n_tm)]
+    if direct:
+        all_partners = [
+            {"tm": tms[t], "lat": lats[d]}
+            for t in range(n_tm) for d in range(n_lat) if t or d
+        ]
+        partners = all_partners
+    else:
+        partners = lat_partners + tm_partners
     barrier = pltpu.get_barrier_semaphore()
-    if direct:
-        partners = [all_partner(d) for d in range(1, n_dev)]
-    else:
-        partners = [lat_partner(d) for d in range(1, n_lat)]
-        partners += [tm_partner(d) for d in range(1, n_tm)]
     for partner in partners:
         pl.semaphore_signal(barrier, inc=1, device_id=partner, device_id_type=MESH)
+
+    own = slice(0, rows)
+    loads = []
+
+    def load(src, dst):
+        copy = pltpu.make_async_copy(src, dst, lsem.at[len(loads)])
+        copy.start()
+        loads.append(copy)
+
+    load(states_hbm.at[0], xs.at[0, :, own])
+    load(mask_hbm, land_mask)
+    load(error_hbm, error_std)
+    load(cells_hbm, obs_cells)
+    load(moments_hbm, obs_moments)
+    load(values_hbm, obs_values)
+    load(obs_err_hbm, obs_error)
+    for it in range(ITERS):
+        @pl.when(tm == 0)
+        def _(it=it):
+            pltpu.make_async_copy(background_hbm, fe_prev.at[it], lsem.at[7 + it]).start()
 
     def remote(src, dst, k, device):
         return pltpu.make_async_remote_copy(
@@ -102,20 +123,21 @@
         )
 
     pending = []
-
-    def send(cond, src, dst, k, device):
+    late = []
+
+    def send(cond, src, dst, k, device, queue=pending):
         @pl.when(cond)
         def _():
             remote(src, dst, k, device).start()
 
-        pending.append((cond, src, k, device))
-
-    def drain():
-        for cond, src, k, device in pending:
+        queue.append((cond, src, k, device))
+
+    def drain(queue):
+        for cond, src, k, device in queue:
             @pl.when(cond)
             def _(src=src, k=k, device=device):
                 remote(src, src, k, device).wait_send()
-        pending.clear()
+        queue.clear()
 
     def arrive(cond, dst, k, device):
         @pl.when(cond)
@@ -125,7 +147,6 @@
     zeros_half = jnp.zeros((3, half, lon), jnp.float32)
     lo, hi = slice(0, half), slice(half, rows)
     lo_w, hi_w = slice(rows, rows + half), slice(rows + half, wide)
-    own = slice(0, rows)
 
     @pl.when(lat == n_lat - 1)
     def _():
@@ -149,11 +170,7 @@
         for it in range(ITERS):
             dir_next[it] = jnp.zeros(xnext.shape, jnp.float32)
 
-    @pl.when(tm == 0)
-    def _():
-        for it in range(ITERS):
-            fe_prev[it] = background[...]
-
+    loads[1].wait()
     mask = land_mask[...].astype(jnp.float32)
     tile_cols = mask.shape[1]
     masks[own, :] = jnp.concatenate(
@@ -161,15 +178,17 @@
         axis=0,
     )
 
+    loads[0].wait()
     pl.semaphore_wait(barrier, len(partners))
 
     send(has_up, masks.at[lo], masks.at[lo_w], 0, up)
     send(has_down, masks.at[hi], masks.at[hi_w], 1, down)
-    send(has_up, states.at[0, :, lo], xs.at[0, :, lo_w], 2, up)
-    send(has_down, states.at[0, :, hi], xs.at[0, :, hi_w], 3, down)
-    send(has_prev, states.at[0], xnext, 4, before)
-
-    xs[0, :, own, :] = states[0]
+    send(has_up, xs.at[0, :, lo], xs.at[0, :, lo_w], 2, up)
+    send(has_down, xs.at[0, :, hi], xs.at[0, :, hi_w], 3, down)
+    send(has_prev, xs.at[0, :, own], xnext, 4, before)
+
+    for copy in loads[2:]:
+        copy.wait()
     var = error_std[...] * error_std[...]
     variance[...] = var
     inv_var[...] = 1.0 / var
@@ -307,16 +326,16 @@
 
     def exchange(buf, value, k, size, mine, partner):
         buf[mine] = value
-        for d in range(1, size):
-            remote(buf.at[mine], buf.at[mine], k, partner(d)).start()
+        for device in partner:
+            remote(buf.at[mine], buf.at[mine], k, device).start()
 
     def collect(buf, k, size, partner):
-        remote(buf.at[0 : size - 1], buf.at[0 : size - 1], k, partner(1)).wait_recv()
+        remote(buf.at[0 : size - 1], buf.at[0 : size - 1], k, partner[0]).wait_recv()
         total = jnp.sum(buf[...], axis=0)
         return total
 
     def sent(buf, k, size, partner):
-        remote(buf.at[0 : size - 1], buf.at[0 : size - 1], k, partner(1)).wait_send()
+        remote(buf.at[0 : size - 1], buf.at[0 : size - 1], k, partner[0]).wait_send()
 
     scale = None
     for it in range(ITERS):
@@ -358,6 +377,11 @@
         send(has_up, lam.at[0, :, hi_w], adj_in.at[it, :, hi], base + 2, up)
 
         arrive(has_prev, fe_prev.at[it], base, before)
+
+        @pl.when(tm == 0)
+        def _():
+            pltpu.make_async_copy(background_hbm, fe_prev.at[it], lsem.at[7 + it]).wait()
+
         cost = misfit * weighted
         for f in range(3):
             gap = xs[0, f, own, :] - fe_prev[it, f]
@@ -373,19 +397,20 @@
 
         message = jnp.concatenate([steep, cost], axis=0)
         if direct:
-            exchange(parts.at[it], message, base + 6, n_dev, me, all_partner)
+            exchange(parts.at[it], message, base + 6, n_dev, me, all_partners)
         else:
-            exchange(parts.at[it], message, base + 6, n_lat, lat, lat_partner)
-        send(has_up, dir_buf.at[it, :, lo], dir_halo.at[it, :, lo], base + 3, up)
-        send(has_down, dir_buf.at[it, :, hi], dir_halo.at[it, :, hi], base + 4, down)
+            exchange(parts.at[it], message, base + 6, n_lat, lat, lat_partners)
+        send(has_up, dir_buf.at[it, :, lo], dir_halo.at[it, :, lo], base + 3, up, late)
+        send(has_down, dir_buf.at[it, :, hi], dir_halo.at[it, :, hi], base + 4, down, late)
+        drain(pending)
         if direct:
-            send(has_prev, dir_buf.at[it], dir_next.at[it], base + 5, before)
-            total = collect(parts.at[it], base + 6, n_dev, all_partner)
+            send(has_prev, dir_buf.at[it], dir_next.at[it], base + 5, before, late)
+            total = collect(parts.at[it], base + 6, n_dev, all_partners)
         else:
-            total = collect(parts.at[it], base + 6, n_lat, lat_partner)
-            exchange(parts_tm.at[it], total, base + 7, n_tm, tm, tm_partner)
-            send(has_prev, dir_buf.at[it], dir_next.at[it], base + 5, before)
-            total = collect(parts_tm.at[it], base + 7, n_tm, tm_partner)
+            total = collect(parts.at[it], base + 6, n_lat, lat_partners)
+            exchange(parts_tm.at[it], total, base + 7, n_tm, tm, tm_partners)
+            send(has_prev, dir_buf.at[it], dir_next.at[it], base + 5, before, late)
+            total = collect(parts_tm.at[it], base + 7, n_tm, tm_partners)
         steepness = jnp.sum(total[0:1], axis=1, keepdims=True)
         scale = STEP_LENGTH / jnp.sqrt(steepness / (n_tm * cell_count) + EPSILON)
         costs_out[it] = jnp.sum(total[1:2]) * (0.5 / cell_count)
@@ -396,24 +421,48 @@
         arrive(has_up, dir_halo.at[it, :, hi], base + 4, up)
         for f in range(3):
             xs[0, f, rows:wide, :] = xs[0, f, rows:wide, :] - scale * dir_halo[it, f]
-        drain()
-        if direct:
-            sent(parts.at[it], base + 6, n_dev, all_partner)
-        else:
-            sent(parts.at[it], base + 6, n_lat, lat_partner)
-            sent(parts_tm.at[it], base + 7, n_tm, tm_partner)
-
-    est_out[0] = xs[0, :, own, :]
+
+    est_copy = pltpu.make_async_copy(
+        xs.at[0, :, own], est_out.at[0], lsem.at[7 + ITERS]
+    )
+    est_copy.start()
     lax.fori_loop(0, STEPS, forward_step, 0)
     arrive(has_next, dir_next.at[ITERS - 1], 5 + 8 * (ITERS - 1) + 5, after)
 
     @pl.when(has_next)
     def _():
-        slid_out[0] = xnext[...] - scale * dir_next[ITERS - 1]
+        xnext[...] = xnext[...] - scale * dir_next[ITERS - 1]
 
     @pl.when(tm == n_tm - 1)
     def _():
-        slid_out[0] = xs[STEPS, :, own, :]
+        xnext[...] = xs[STEPS, :, own, :]
+
+    slid_copy = pltpu.make_async_copy(xnext, slid_out.at[0], lsem.at[8 + ITERS])
+    slid_copy.start()
+    est_copy.wait()
+    slid_copy.wait()
+    drain(late)
+    for it in range(ITERS):
+        base = 5 + 8 * it
+        if direct:
+            sent(parts.at[it], base + 6, n_dev, all_partners)
+        else:
+            sent(parts.at[it], base + 6, n_lat, lat_partners)
+            sent(parts_tm.at[it], base + 7, n_tm, tm_partners)
+
+
+def write_out(est, slid, costs, est_out, slid_out, costs_out, est_v, slid_v, costs_s, sem):
+    moves = []
+    for i, (src, held) in enumerate(((est, est_v), (slid, slid_v), (costs, costs_s))):
+        moves.append(pltpu.make_async_copy(src, held, sem.at[i]))
+        moves[-1].start()
+    outs = []
+    for i, (held, dst) in enumerate(((est_v, est_out), (slid_v, slid_out), (costs_s, costs_out))):
+        moves[i].wait()
+        outs.append(pltpu.make_async_copy(held, dst, sem.at[3 + i]))
+        outs[-1].start()
+    for copy in outs:
+        copy.wait()
 
 
 def shards(n_tm, n_lat, *args):
@@ -425,17 +474,17 @@
     direct = n_tm * n_lat <= DIRECT_MAX
     field = (3, rows, lon)
     sems = 5 + 8 * ITERS
-    return pl.pallas_call(
+    est, slid, costs = pl.pallas_call(
         functools.partial(kernel, n_tm, n_lat),
         out_shape=(
             jax.ShapeDtypeStruct(states.shape, f32),
             jax.ShapeDtypeStruct(states.shape, f32),
             jax.ShapeDtypeStruct((ITERS,), f32),
         ),
-        in_specs=[pl.BlockSpec(memory_space=pltpu.VMEM)] * 8,
+        in_specs=[pl.BlockSpec(memory_space=pltpu.HBM)] * 8,
         out_specs=(
-            pl.BlockSpec(memory_space=pltpu.VMEM),
-            pl.BlockSpec(memory_space=pltpu.VMEM),
+            pl.BlockSpec(memory_space=pltpu.HBM),
+            pl.BlockSpec(memory_space=pltpu.HBM),
             pl.BlockSpec(memory_space=pltpu.SMEM),
         ),
         scratch_shapes=[
@@ -457,13 +506,36 @@
             pltpu.VMEM((ITERS,) + field, f32),
             pltpu.VMEM((ITERS, n_tm * n_lat if direct else n_lat, 2, LANES), f32),
             pltpu.VMEM((ITERS, n_tm, 2, LANES), f32),
+            pltpu.VMEM(field, f32),
+            pltpu.VMEM(args[3].shape, jnp.int32),
+            pltpu.VMEM((1, n_obs), jnp.int32),
+            pltpu.VMEM((1, n_obs), jnp.int32),
+            pltpu.VMEM((1, n_obs), f32),
+            pltpu.VMEM((1, n_obs), f32),
             pltpu.SemaphoreType.DMA((sems,)),
             pltpu.SemaphoreType.DMA((sems,)),
+            pltpu.SemaphoreType.DMA((9 + ITERS,)),
         ],
         compiler_params=pltpu.CompilerParams(
-            collective_id=0, has_side_effects=True, vmem_limit_bytes=40 * 1024 * 1024
+            collective_id=0, has_side_effects=True
         ),
     )(*args)
+    return pl.pallas_call(
+        write_out,
+        out_shape=(
+            jax.ShapeDtypeStruct(states.shape, f32),
+            jax.ShapeDtypeStruct(states.shape, f32),
+            jax.ShapeDtypeStruct((ITERS,), f32),
+        ),
+        in_specs=[pl.BlockSpec(memory_space=pltpu.HBM)] * 3,
+        out_specs=(pl.BlockSpec(memory_space=pltpu.HBM),) * 3,
+        scratch_shapes=[
+            pltpu.VMEM(states.shape, f32),
+            pltpu.VMEM(states.shape, f32),
+            pltpu.SMEM((ITERS,), f32),
+            pltpu.SemaphoreType.DMA((6,)),
+        ],
+    )(est, slid, costs)
 
 
 def solution(mesh):

time: 48.4 us -> 43.2 us (0.89)
  local copies, waits for them, and re-layouts: 7.94 us -> 0 us
  Pallas kernels: 39.5 us -> 42.4 us
    unnamed x19 -> x0, local copies, waits for them, and re-layouts: 7.94 us -> none
    pallas_call x0 -> x1, Pallas kernels: none -> 1.76 us  [shards(): pl.pallas_call(write_out, out_shape=(jax.ShapeDtypeStruct(states.shape, f...]
    pallas_call x1, Pallas kernels: 39.5 us -> 40.7 us  [shards(): pl.pallas_call(functools.partial(kernel, n_tm, n_lat), out_shape=(jax.Sha...]
where the time goes in v2:
time: 43.2 us; the launch traced here: 43.1 us
  Pallas kernels  42.4 us (98%)
  between operations  0.64 us (1%)
    pallas_call x1, Pallas kernels, shards(): pl.pallas_call(functools.partial(kernel, n_tm, n_lat), out_shape=(jax.Sha...  40.7 us
    pallas_call x1, Pallas kernels, shards(): pl.pallas_call(write_out, out_shape=(jax.ShapeDtypeStruct(states.shape, f...  1.76 us

profile of v2, /device:TPU:0, one launch (start us, length us, event | category | flops | bytes accessed | tf_op | source)
XLA Modules:
  0.0 43.1 jit_solution(7779605791093140958)
XLA Ops:
  0.6 40.7 %shard_map.103 = (f32[1,3,8,2048]{3,2,1,0:T(8,128)}, f32[1,3,8,2048]{3,2,1,0:T(8,128)}, f32[2]{0:T(128)}) custom-call(f32[1,3,8,2048]{3,2,1,0:T(8,128)} %states_hbm.1, f32[3,8,2048]{2,1,0:T(8,128)} %background_hbm.1, f32[3,8,2048]{2,1,0:T(8,128)} %error_hbm.1, s32[2,128]{1,0:T(2,128)} %mask_hbm.1, s32[1,128]{1,0:T(1,128)} %cells_hbm.1, ...), custom_call_target="tpu_custom_call" | custom-call | tf_op jit(solution)/shard_map/pallas_call | solution.py:477
  41.3 1.8 %shard_map.104 = (f32[1,3,8,2048]{3,2,1,0:T(8,128)}, f32[1,3,8,2048]{3,2,1,0:T(8,128)}, f32[2]{0:T(128)}) custom-call(f32[1,3,8,2048]{3,2,1,0:T(8,128)} %get-tuple-element.6.est, f32[1,3,8,2048]{3,2,1,0:T(8,128)} %get-tuple-element.7.slid, f32[2]{0:T(128)} %get-tuple-element.8.costs), custom_call_target="tpu_custom_call" | custom-call | tf_op jit(solution)/shard_map/pallas_call | solution.py:523

commit v3 on v2

--- a/solution.py
+++ b/solution.py
@@ -22,7 +22,7 @@
 
 MESH = pl.DeviceIdType.MESH
 LANES = 128
-WIDTH = 512
+WIDTH = 1024
 DIRECT_MAX = 64
 
 

time: 43.2 us -> 42.1 us (0.975)
  Pallas kernels: 42.4 us -> 41.3 us
    pallas_call x1, Pallas kernels: 40.7 us -> 39.6 us  [shards(): pl.pallas_call(functools.partial(kernel, n_tm, n_lat), out_shape=(jax.Sha...]
where the time goes in v3:
time: 42.1 us; the launch traced here: 42 us
  Pallas kernels  41.3 us (98%)
  between operations  0.64 us (2%)
    pallas_call x1, Pallas kernels, shards(): pl.pallas_call(functools.partial(kernel, n_tm, n_lat), out_shape=(jax.Sha...  39.6 us
    pallas_call x1, Pallas kernels, shards(): pl.pallas_call(write_out, out_shape=(jax.ShapeDtypeStruct(states.shape, f...  1.76 us

profile of v3, /device:TPU:0, one launch (start us, length us, event | category | flops | bytes accessed | tf_op | source)
XLA Modules:
  0.0 42.0 jit_solution(2055993408269769140)
XLA Ops:
  0.6 39.6 %shard_map.103 = (f32[1,3,8,2048]{3,2,1,0:T(8,128)}, f32[1,3,8,2048]{3,2,1,0:T(8,128)}, f32[2]{0:T(128)}) custom-call(f32[1,3,8,2048]{3,2,1,0:T(8,128)} %states_hbm.1, f32[3,8,2048]{2,1,0:T(8,128)} %background_hbm.1, f32[3,8,2048]{2,1,0:T(8,128)} %error_hbm.1, s32[2,128]{1,0:T(2,128)} %mask_hbm.1, s32[1,128]{1,0:T(1,128)} %cells_hbm.1, ...), custom_call_target="tpu_custom_call" | custom-call | tf_op jit(solution)/shard_map/pallas_call | solution.py:477
  40.2 1.8 %shard_map.104 = (f32[1,3,8,2048]{3,2,1,0:T(8,128)}, f32[1,3,8,2048]{3,2,1,0:T(8,128)}, f32[2]{0:T(128)}) custom-call(f32[1,3,8,2048]{3,2,1,0:T(8,128)} %get-tuple-element.6.est, f32[1,3,8,2048]{3,2,1,0:T(8,128)} %get-tuple-element.7.slid, f32[2]{0:T(128)} %get-tuple-element.8.costs), custom_call_target="tpu_custom_call" | custom-call | tf_op jit(solution)/shard_map/pallas_call | solution.py:523
